TPU v7x, 512 devices: a whole 4x8x8 slice. The times are simulated.
512 devices in a mesh: replica: 32 (over y, x), owner: 16 (over z, core).
Axes of the slice: x: 4, y: 8, z: 8, core: 2. Of those that a mesh axis runs over, the one named last changes fastest.
Arguments:
- owner_of: int32 [24], replicated, may hold values from 0 to 15, as said below
- grad: bfloat16 [32, 32, 2304, 128], P('replica', 'owner')
- error: bfloat16 [32, 32, 2304, 128], P('replica', 'owner'), may hold values from -4 to 4
- q_prev: float32 [32, 128, 32], P('owner')
- weight: float32 [32, 2304, 128], P('owner', 'replica'), may hold values from -0.125 to 0.125
- momentum: float32 [32, 2304, 128], P('owner', 'replica'), may hold values from -1.2 to 1.2
- vec_grad: bfloat16 [32, 128, 2304], P('replica', 'owner')
- vec_weight: float32 [128, 2304], P('owner', 'replica'), may hold values from 0.5 to 1.5
- vec_mom: float32 [128, 2304], P('owner', 'replica'), may hold values from -1.2 to 1.2
Outputs:
- weight_next: float32 [32, 2304, 128], P('owner', 'replica')
- momentum_next: float32 [32, 2304, 128], P('owner', 'replica')
- error_next: bfloat16 [32, 32, 2304, 128], P('replica', 'owner')
- q_next: float32 [32, 128, 32], P('owner')
- vec_weight_next: float32 [128, 2304], P('owner', 'replica')
- vec_mom_next: float32 [128, 2304], P('owner', 'replica')
Inputs may be any that keep to these rules, and one draw needn't show every extreme that they name: `owner_of`: every owner index appears once or twice; half of them appear twice.
All inputs are finite; a program needn't handle non-finite values.
Results may differ from a plain program's by a relative error of at most 0.001.
Values sent between devices are 32-bit elements; how exact they have to be, the bound alone decides.
A program may use at most 64 MiB of HBM per device.

v0:
```python
import jax
import jax.numpy as jnp
from jax import lax
from jax.sharding import PartitionSpec as P

NS_ITERS = 5
exact_mode = lax.Precision.HIGHEST
clip_limit = 0.1
momentum_decay = 0.9
learn_rate = 0.05


def inverse_root(gram_mat, iterations):
    identity = jnp.eye(gram_mat.shape[-1], dtype=jnp.float32)
    scale_sq = jnp.sqrt(jnp.sum(gram_mat * gram_mat, axis=(1, 2), keepdims=True) + 1e-06)
    current = gram_mat / scale_sq
    inv_root = jnp.broadcast_to(identity, gram_mat.shape)
    for iteration in range(iterations):
        factor_mat = 1.5 * identity - 0.5 * jnp.einsum(
            "sij,sjk->sik", inv_root, current, precision=exact_mode
        )
        current = jnp.einsum("sij,sjk->sik", current, factor_mat, precision=exact_mode)
        inv_root = jnp.einsum("sij,sjk->sik", factor_mat, inv_root, precision=exact_mode)
    return (inv_root, scale_sq)


def on_device(owner_of, grad, error, q_prev, weight, momentum, vec_grad, vec_weight, vec_mom):
    replicas = lax.axis_size("replica")
    owners = lax.axis_size("owner")
    rank_index = lax.axis_index("replica")
    owner_index = lax.axis_index("owner")
    slot_count = grad.shape[1]
    rows_share = weight.shape[1]
    count_own = jnp.sum((owner_of == owner_index).astype(jnp.int32))
    live_slots = jnp.arange(slot_count, dtype=jnp.int32) < count_own
    live_mask = live_slots[:, None, None]
    merged = grad[0].astype(jnp.float32) + error[0].astype(jnp.float32)
    left_terms = jnp.einsum("sdw,swk->sdk", merged, q_prev, precision=exact_mode)
    vec_terms = vec_grad[0].astype(jnp.float32)
    p_sum, vec_sum = lax.psum((left_terms, vec_terms), "replica")
    gram_mat = jnp.einsum("sdi,sdj->sij", p_sum, p_sum, precision=exact_mode)
    inv_root, scale_sq = inverse_root(gram_mat, NS_ITERS)
    p_hat = jnp.einsum("sdi,sij->sdj", p_sum, inv_root, precision=exact_mode) / jnp.sqrt(scale_sq)
    vec_full = vec_sum / replicas
    vec_cols = lax.dynamic_slice_in_dim(vec_full, rank_index * rows_share, rows_share, 1)
    right_terms = jnp.einsum("sdw,sdk->swk", merged, p_hat, precision=exact_mode)
    q_new = lax.psum(right_terms, "replica") / replicas
    approx = jnp.einsum("sdk,swk->sdw", p_hat, q_new, precision=exact_mode)
    error_next = jnp.where(live_mask, (merged - approx).astype(jnp.bfloat16), error[0])
    approx_rows = lax.dynamic_slice_in_dim(approx, rank_index * rows_share, rows_share, 1)
    local_sq = jnp.sum(jnp.where(live_mask, approx * approx, 0.0)) + jnp.sum(vec_full * vec_full)
    total_sq = lax.psum(local_sq, "owner")
    width = merged.shape[1]
    entry_count = float(
        owner_of.shape[0] * width * merged.shape[2] + owners * vec_grad.shape[1] * width
    )
    factor = jnp.minimum(1.0, clip_limit / jnp.sqrt(total_sq / entry_count + 1e-06))
    momentum_next = jnp.where(live_mask, momentum_decay * momentum + factor * approx_rows, momentum)
    weight_next = jnp.where(live_mask, weight - learn_rate * momentum_next, weight)
    q_next = jnp.where(live_mask, q_new, q_prev)
    vec_mom_next = momentum_decay * vec_mom + factor * vec_cols
    vec_weight_next = vec_weight - learn_rate * vec_mom_next
    return (weight_next, momentum_next, error_next[None], q_next, vec_weight_next, vec_mom_next)


def solution(mesh):
    return jax.shard_map(
        on_device,
        mesh=mesh,
        in_specs=(
            P(),
            P("replica", "owner", None, None),
            P("replica", "owner", None, None),
            P("owner", None, None),
            P("owner", "replica", None),
            P("owner", "replica", None),
            P("replica", "owner", None),
            P("owner", "replica"),
            P("owner", "replica"),
        ),
        out_specs=(
            P("owner", "replica", None),
            P("owner", "replica", None),
            P("replica", "owner", None, None),
            P("owner", None, None),
            P("owner", "replica"),
            P("owner", "replica"),
        ),
        check_vma=False,
    )
```

profile of v0, /device:TPU:1, one launch (start us, length us, event | category | flops | bytes accessed | tf_op | source)
XLA Modules:
  0.0 373.0 jit_solution(3170516663309399154)
XLA Ops:
  7.2 1.4 bitcast_convert_fusion
  8.6 5.1 %fusion.1 = f32[2,2304,32]{1,2,0:T(8,128)} fusion(f32[2,128,32]{1,2,0:T(8,128)} %param.12, bf16[1,2,2304,128]{3,2,1,0:T(8,128)(2,1)} %param.10, bf16[1,2,2304,128]{3,2,1,0:T(8,128)(2,1)} %param.11), kind=kOutput, calls=%fused_computation.5 | convolution fusion | flops 228261888 | bytes 2981888 | tf_op jit(solution)/shard_map/sdw,swk->sdk/dot_general | solution.py:38
  13.8 0.6 fusion.22
  14.4 0.6 iota_compare_fusion.1
  15.1 159.0 %all-reduce.3.cloned.1.call-done = (f32[2,2304,32]{1,2,0:T(8,128)}, f32[8,2304]{1,0:T(8,128)}) async-done(((f32[2,2304,32]{1,2,0:T(8,128)}, f32[8,2304]{1,0:T(8,128)}), (f32[2,2304,32]{1,2,0:T(8,128)}, f32[8,2304]{1,0:T(8,128)})) %all-reduce.3.cloned.1.call-update) | async-done | bytes 663568 | tf_op jit(solution)/shard_map/psum | solution.py:40
  174.1 2.1 multiply_reduce_fusion.1
  176.2 0.2 fusion.12
  176.5 0.2 fusion.21
  176.9 0.2 fusion.11
  177.1 0.2 fusion.26
  177.4 0.2 fusion.10
  177.9 0.2 fusion.9
  178.4 0.6 broadcast_multiply_fusion
  179.1 0.2 fusion.8
  179.2 0.2 fusion.31
  179.5 0.6 convolution_divide_fusion
  180.1 1.6 fusion
  181.8 113.6 %psum.29 = f32[2,128,32]{1,2,0:T(8,128)S(1)} all-reduce(f32[2,128,32]{1,2,0:T(8,128)S(1)} %fusion), channel_id=1, replica_groups=mesh['replica'=32,'owner'=16] {'replica'}, use_global_device_ids=true, to_apply=%region_3.0 | all-reduce | flops 8192 | bytes 65536 | tf_op jit(solution)/shard_map/psum | solution.py:47
  295.4 5.9 %select_reduce_fusion = (f32[]{:T(128)}, f32[2,2304,128]{2,1,0:T(8,128)}) fusion(pred[2]{0:T(512)(128)(4,1)S(1)} %iota_compare_fusion.1, f32[2,2304,32]{1,2,0:T(8,128)S(1)} %convolution_divide_fusion, f32[2,128,32]{1,2,0:T(8,128)S(1)} %psum.29), kind=kOutput, calls=%fused_computation.3 | convolution fusion | flops 228270080 | bytes 2981894 | tf_op jit(solution)/shard_map/sdk,swk->sdw/dot_general | solution.py:48
  302.6 0.7 multiply_select_fusion
  303.3 56.5 %psum.31 = f32[]{:T(128)} all-reduce(f32[]{:T(128)S(6)} %add.40), channel_id=1, replica_groups=mesh['replica'=32,'owner'=16] {'owner'}, use_global_device_ids=true, to_apply=%region_7.8 | all-reduce | flops 1 | bytes 8 | tf_op jit(solution)/shard_map/psum | solution.py:52
  360.6 3.2 fusion.3
  363.8 1.6 subtract_select_fusion
  365.5 0.7 multiply_subtract_fusion
  (31 shorter events, 1.1 us)
Async XLA Ops:
  7.2 6.6 %copy-start.9 = (s32[24]{0:T(128)S(1)}, s32[24]{0:T(128)}, u32[]{:S(2)}) copy-start(s32[24]{0:T(128)} %param.9) | copy-start | bytes 292
  7.2 166.9 %all-reduce.3.cloned.1.call-start = ((), (), s32[]{:S(2)}) async-start(), calls=%async_computation | async-start | bytes 1327104 | tf_op jit(solution)/shard_map/psum | solution.py:40
  174.1 4.4 %copy-start.4 = (f32[8,2304]{1,0:T(8,128)S(1)}, f32[8,2304]{1,0:T(8,128)}, u32[]{:S(2)}) copy-start(f32[8,2304]{1,0:T(8,128)} %get-tuple-element.7) | copy-start | bytes 221188
  174.1 5.4 %copy-start.2 = (f32[2,2304,32]{1,2,0:T(8,128)S(1)}, f32[2,2304,32]{1,2,0:T(8,128)}, u32[]{:S(2)}) copy-start(f32[2,2304,32]{1,2,0:T(8,128)} %get-tuple-element.6) | copy-start | bytes 1769476
  174.1 6.0 %copy-start = (bf16[1,2,2304,128]{3,2,1,0:T(8,128)(2,1)S(1)}, bf16[1,2,2304,128]{3,2,1,0:T(8,128)(2,1)}, u32[]{:S(2)}) copy-start(bf16[1,2,2304,128]{3,2,1,0:T(8,128)(2,1)} %param.10) | copy-start | bytes 3538948
  174.1 6.0 %copy-start.1 = (bf16[1,2,2304,128]{3,2,1,0:T(8,128)(2,1)S(1)}, bf16[1,2,2304,128]{3,2,1,0:T(8,128)(2,1)}, u32[]{:S(2)}) copy-start(bf16[1,2,2304,128]{3,2,1,0:T(8,128)(2,1)} %param.11) | copy-start | bytes 3538948
  180.1 122.5 %copy-start.3 = (f32[2,128,32]{1,2,0:T(8,128)S(1)}, f32[2,128,32]{1,2,0:T(8,128)}, u32[]{:S(2)}) copy-start(f32[2,128,32]{1,2,0:T(8,128)} %param.12) | copy-start | bytes 98308
  360.5 3.3 copy-start.5
  360.5 3.3 copy-start.6
  360.6 4.9 %copy-start.7 = (f32[8,72]{1,0:T(8,128)S(1)}, f32[8,72]{1,0:T(8,128)}, u32[]{:S(2)}) copy-start(f32[8,72]{1,0:T(8,128)} %param.16) | copy-start | bytes 6916
  360.6 4.9 %copy-start.8 = (f32[8,72]{1,0:T(8,128)S(1)}, f32[8,72]{1,0:T(8,128)}, u32[]{:S(2)}) copy-start(f32[8,72]{1,0:T(8,128)} %param.17) | copy-start | bytes 6916
Sparse Core Ops, SparseCore 0:
  13.9 160.1 all-reduce.2
where the time goes:
time: 373 us
  blocking collectives  170 us (46%)
  waiting for transfers between devices  159 us (43%)
  matrix products  17.9 us (5%)
  between operations  16.3 us (4%)
  other arithmetic  9.55 us (3%)
    psum x1, waiting for transfers between devices, on_device(): p_sum, vec_sum = lax.psum((left_terms, vec_terms), 'replica')  159 us
    psum x1, blocking collectives, on_device(): q_new = lax.psum(right_terms, 'replica') / replicas  114 us
    psum x1, blocking collectives, on_device(): total_sq = lax.psum(local_sq, 'owner')  56.5 us
  transfers between devices with their start and end apart: 1, of which 1 were waited for; matrix products, arithmetic and copies ran while one was open for 0% of the time, Pallas kernels for 0%

commit v1 on v0

--- a/solution.py
+++ b/solution.py
@@ -44,7 +44,7 @@
     vec_full = vec_sum / replicas
     vec_cols = lax.dynamic_slice_in_dim(vec_full, rank_index * rows_share, rows_share, 1)
     right_terms = jnp.einsum("sdw,sdk->swk", merged, p_hat, precision=exact_mode)
-    q_new = lax.psum(right_terms, "replica") / replicas
+    q_new = jnp.sum(lax.all_gather(right_terms, "replica"), axis=0) / replicas
     approx = jnp.einsum("sdk,swk->sdw", p_hat, q_new, precision=exact_mode)
     error_next = jnp.where(live_mask, (merged - approx).astype(jnp.bfloat16), error[0])
     approx_rows = lax.dynamic_slice_in_dim(approx, rank_index * rows_share, rows_share, 1)

time: 373 us -> 314 us (0.84)
  blocking collectives: 170 us -> 29.5 us
  waiting for transfers between devices: 159 us -> 238 us
    psum x1 -> x0, blocking collectives: 114 us -> none  [on_device(): q_new = lax.psum(right_terms, 'replica') / replicas]
    all_gather x0 -> x1, waiting for transfers between devices: none -> 77.5 us  [on_device(): q_new = jnp.sum(lax.all_gather(right_terms, 'replica'), axis=0) / replicas]
    psum x1, blocking collectives: 56.5 us -> 29.5 us  [on_device(): total_sq = lax.psum(local_sq, 'owner')]
  transfers between devices with their start and end apart: 1 -> 2, of which waited for: 1 -> 2; matrix products, arithmetic and copies ran while one was open for 0% -> 1% of each run, Pallas kernels for 0% -> 0%
where the time goes in v1:
time: 314 us
  waiting for transfers between devices  238 us (76%)
  blocking collectives  29.5 us (9%)
  matrix products  19.5 us (6%)
  between operations  16.3 us (5%)
  other arithmetic  10.8 us (3%)
    psum x1, waiting for transfers between devices, on_device(): p_sum, vec_sum = lax.psum((left_terms, vec_terms), 'replica')  160 us
    all_gather x1, waiting for transfers between devices, on_device(): q_new = jnp.sum(lax.all_gather(right_terms, 'replica'), axis=0) / replicas  77.5 us
    psum x1, blocking collectives, on_device(): total_sq = lax.psum(local_sq, 'owner')  29.5 us
  transfers between devices with their start and end apart: 2, of which 2 were waited for; matrix products, arithmetic and copies ran while one was open for 1% of the time, Pallas kernels for 0%

profile of v1, /device:TPU:1, one launch (start us, length us, event | category | flops | bytes accessed | tf_op | source)
XLA Modules:
  0.0 314.0 jit_solution(10600976711058946783)
XLA Ops:
  7.2 1.4 bitcast_convert_fusion
  8.6 5.1 %fusion.1 = f32[2,2304,32]{1,2,0:T(8,128)} fusion(f32[2,128,32]{1,2,0:T(8,128)} %param.12, bf16[1,2,2304,128]{3,2,1,0:T(8,128)(2,1)} %param.10, bf16[1,2,2304,128]{3,2,1,0:T(8,128)(2,1)} %param.11), kind=kOutput, calls=%fused_computation.5 | convolution fusion | flops 228261888 | bytes 2981888 | tf_op jit(solution)/shard_map/sdw,swk->sdk/dot_general | solution.py:38
  13.8 160.2 %all-reduce.3.cloned.1.call-done = (f32[2,2304,32]{1,2,0:T(8,128)}, f32[8,2304]{1,0:T(8,128)}) async-done(((f32[2,2304,32]{1,2,0:T(8,128)}, f32[8,2304]{1,0:T(8,128)}), (f32[2,2304,32]{1,2,0:T(8,128)}, f32[8,2304]{1,0:T(8,128)})) %all-reduce.3.cloned.1.call-update) | async-done | bytes 663568 | tf_op jit(solution)/shard_map/psum | solution.py:40
  174.1 2.0 multiply_reduce_fusion.1
  176.1 0.2 fusion.12
  176.3 0.2 fusion.21
  176.7 0.2 fusion.11
  177.2 0.2 fusion.10
  177.7 0.2 fusion.9
  178.3 0.2 fusion.8
  178.4 0.2 fusion.31
  178.7 1.7 convolution_divide_fusion
  180.4 2.3 fusion
  182.7 0.6 fusion.22
  183.4 0.6 iota_compare_fusion.1
  184.0 0.6 broadcast_multiply_fusion
  184.7 77.5 %all-gather.3.cloned.1.call-done = f32[64,128,32]{1,2,0:T(8,128)} async-done(((f32[2,128,32]{1,2,0:T(8,128)}), f32[64,128,32]{1,2,0:T(8,128)}) %all-gather.3.cloned.1.call-update) | async-done | bytes 1048592 | tf_op jit(solution)/shard_map/all_gather | solution.py:47
  262.2 1.3 reduce_sum.47
  263.5 5.9 %select_reduce_fusion = (f32[]{:T(128)}, f32[2,2304,128]{2,1,0:T(8,128)}) fusion(pred[2]{0:T(512)(128)(4,1)S(1)} %iota_compare_fusion.1, f32[2,2304,32]{1,2,0:T(8,128)S(1)} %convolution_divide_fusion, f32[2,128,32]{1,2,0:T(8,128)S(1)} %reduce_sum.47), kind=kOutput, calls=%fused_computation.3 | convolution fusion | flops 228270080 | bytes 2981894 | tf_op jit(solution)/shard_map/sdk,swk->sdw/dot_general | solution.py:48
  270.7 0.7 multiply_select_fusion
  271.4 29.5 %psum.23 = f32[]{:T(128)} all-reduce(f32[]{:T(128)S(6)} %add.38), channel_id=1, replica_groups=mesh['replica'=32,'owner'=16] {'owner'}, use_global_device_ids=true, to_apply=%region_7.8 | all-reduce | flops 1 | bytes 8 | tf_op jit(solution)/shard_map/psum | solution.py:52
  301.6 3.2 %fusion.3 = bf16[1,2,2304,128]{3,2,1,0:T(8,128)(2,1)} fusion(f32[2,2304,128]{2,1,0:T(8,128)} %get-tuple-element.19, bf16[1,2,2304,128]{3,2,1,0:T(8,128)(2,1)S(1)} %copy-done, bf16[1,2,2304,128]{3,2,1,0:T(8,128)(2,1)S(1)} %copy-done.1, pred[2]{0:T(512)(128)(4,1)S(1)} %iota_compare_fusion.1), kind=kLoop, calls=%fused_computation.7 | loop fusion | flops 3538944 | bytes 5898242 | tf_op jit(solution)/shard_map/broadcast_in_dim | solution.py:63
  304.9 1.6 subtract_select_fusion
  306.5 0.7 multiply_subtract_fusion
  (32 shorter events, 1.3 us)
Async XLA Ops:
  7.2 166.9 %all-reduce.3.cloned.1.call-start = ((), (), s32[]{:S(2)}) async-start(), calls=%async_computation.1 | async-start | bytes 1327104 | tf_op jit(solution)/shard_map/psum | solution.py:40
  13.7 248.4 %all-gather.3.cloned.1.call-start = ((), (), s32[]{:S(2)}) async-start(), calls=%async_computation | async-start | bytes 1081344 | tf_op jit(solution)/shard_map/all_gather | solution.py:47
  13.8 166.6 %copy-start = (bf16[1,2,2304,128]{3,2,1,0:T(8,128)(2,1)S(1)}, bf16[1,2,2304,128]{3,2,1,0:T(8,128)(2,1)}, u32[]{:S(2)}) copy-start(bf16[1,2,2304,128]{3,2,1,0:T(8,128)(2,1)} %param.10) | copy-start | bytes 3538948
  13.8 166.6 %copy-start.1 = (bf16[1,2,2304,128]{3,2,1,0:T(8,128)(2,1)S(1)}, bf16[1,2,2304,128]{3,2,1,0:T(8,128)(2,1)}, u32[]{:S(2)}) copy-start(bf16[1,2,2304,128]{3,2,1,0:T(8,128)(2,1)} %param.11) | copy-start | bytes 3538948
  178.7 4.1 %copy-start.8 = (s32[24]{0:T(128)S(1)}, s32[24]{0:T(128)}, u32[]{:S(2)}) copy-start(s32[24]{0:T(128)} %param.9) | copy-start | bytes 292
  178.7 5.4 %copy-start.3 = (f32[8,2304]{1,0:T(8,128)S(1)}, f32[8,2304]{1,0:T(8,128)}, u32[]{:S(2)}) copy-start(f32[8,2304]{1,0:T(8,128)} %get-tuple-element.7) | copy-start | bytes 221188
  182.7 88.0 %copy-start.2 = (f32[2,128,32]{1,2,0:T(8,128)S(1)}, f32[2,128,32]{1,2,0:T(8,128)}, u32[]{:S(2)}) copy-start(f32[2,128,32]{1,2,0:T(8,128)} %param.12) | copy-start | bytes 98308
  301.6 3.3 %copy-start.4 = (f32[2,72,128]{2,1,0:T(8,128)S(1)}, f32[2,72,128]{2,1,0:T(8,128)}, u32[]{:S(2)}) copy-start(f32[2,72,128]{2,1,0:T(8,128)} %param.13) | copy-start | bytes 221188
  301.6 3.3 %copy-start.5 = (f32[2,72,128]{2,1,0:T(8,128)S(1)}, f32[2,72,128]{2,1,0:T(8,128)}, u32[]{:S(2)}) copy-start(f32[2,72,128]{2,1,0:T(8,128)} %param.14) | copy-start | bytes 221188
  301.6 4.9 %copy-start.6 = (f32[8,72]{1,0:T(8,128)S(1)}, f32[8,72]{1,0:T(8,128)}, u32[]{:S(2)}) copy-start(f32[8,72]{1,0:T(8,128)} %param.16) | copy-start | bytes 6916
  301.6 4.9 %copy-start.7 = (f32[8,72]{1,0:T(8,128)S(1)}, f32[8,72]{1,0:T(8,128)}, u32[]{:S(2)}) copy-start(f32[8,72]{1,0:T(8,128)} %param.17) | copy-start | bytes 6916
Sparse Core Ops, SparseCore 0:
  13.9 160.1 all-reduce.2
  182.9 79.2 all-gather.2
